TPU v7x, 256 devices: a whole 4x4x8 slice. The times are simulated.
256 devices in a mesh: section: 4 (over x), dp: 64 (over z, y, core).
Axes of the slice: x: 4, y: 4, z: 8, core: 2. Of those that a mesh axis runs over, the one named last changes fastest.
Arguments:
- out_grad: bfloat16 [8192, 5120], P('dp', 'section'), may hold values from -0.26367188 to 0.26367188
- pre_act: bfloat16 [4, 8192, 27648], P('section', 'dp'), may hold values from -6 to 6
- down_a: bfloat16 [4, 27648, 32], P('section'), may hold values from -1 to 1
- down_b: bfloat16 [4, 32, 5120], P('section'), may hold values from -0.078125 to 0.078125
- up_a: bfloat16 [4, 5120, 32], P('section'), may hold values from -1 to 1
- up_b: bfloat16 [4, 27648, 32], P('section'), may hold values from -0.0390625 to 0.0390625
- master: float32 [4, 4, 6912, 32], P('section', None, 'dp'), may hold values from -1 to 1
- moment: float32 [4, 4, 6912, 32], P('section', None, 'dp'), may hold values from -3 to 3
- second: float32 [4, 4, 6912, 32], P('section', None, 'dp'), may hold values from 0.2 to 4
Outputs:
- new_weight: bfloat16 [4, 27648, 32], P('section')
- new_master: float32 [4, 4, 6912, 32], P('section', None, 'dp')
- new_moment: float32 [4, 4, 6912, 32], P('section', None, 'dp')
- new_second: float32 [4, 4, 6912, 32], P('section', None, 'dp')
All inputs are finite; a program needn't handle non-finite values.
Results may differ from a plain program's by a relative error of at most 0.014.
Values may be sent and summed in bfloat16 or wider, within the bound.
No kernel may reach another device: no remote copies, remote signals or barrier semaphores. Data moves between devices by JAX's collectives and lax.ppermute only.
A program may use at most 128 MiB of HBM per device.

v0:
```python
import jax
import jax.numpy as jnp
from jax import lax
from jax.sharding import PartitionSpec as P

BUCKETS = 4
STEP = 20
BETA_ONE = 0.8
BETA_TWO = 0.95
LEARN_RATE = 0.02
DECAY_RATE = 0.1
EPSILON = 1e-08


def shifted(value, axis, steps):
    count = lax.axis_size(axis)
    initial, last = (max(0, -steps), min(count, count - steps))
    return lax.ppermute(value, axis, [(source, source + steps) for source in range(initial, last)])


def slope_of(values):
    sigm = jax.nn.sigmoid(values)
    return sigm * (1.0 + values * (1.0 - sigm))


def adamw(gradient, weights, first, seconds):
    first_new = BETA_ONE * first + (1.0 - BETA_ONE) * gradient
    second_new = BETA_TWO * seconds + (1.0 - BETA_TWO) * gradient * gradient
    first_hat = first_new / (1.0 - BETA_ONE**STEP)
    second_hat = second_new / (1.0 - BETA_TWO**STEP)
    weights_new = weights - LEARN_RATE * (
        first_hat / (jnp.sqrt(second_hat) + EPSILON) + DECAY_RATE * weights
    )
    return (weights_new, first_new, second_new)


def per_device(out_grad, pre_act, down_a, down_b, up_a, up_b, master, moment, second):
    top_grad = lax.all_gather(out_grad, "section", axis=1, tiled=True)
    section_pos = lax.axis_index("section")
    section_count = lax.axis_size("section")
    inputs = pre_act[0].astype(jnp.float32)
    hidden = jax.nn.silu(inputs).astype(jnp.bfloat16)
    slopes = slope_of(inputs)
    factor_a = down_a[0]
    factor_b = down_b[0]
    entry_a = up_a[0]
    entry_b = up_b[0]
    contract_last = (((1,), (1,)), ((), ()))

    def project_low(incoming):
        return lax.dot_general(
            incoming, factor_b, contract_last, preferred_element_type=jnp.float32
        ).astype(jnp.bfloat16)

    current = top_grad
    own_grad = jnp.zeros_like(top_grad)
    for step_index in range(section_count):
        active = section_count - 1 - step_index
        own_grad = jnp.where(section_pos == active, current, own_grad)
        if step_index < section_count - 1:
            low = project_low(current)
            upstream = lax.dot_general(
                low, factor_a, contract_last, preferred_element_type=jnp.float32
            )
            delta = (upstream * slopes).astype(jnp.bfloat16)
            back_low = jnp.dot(delta, entry_b, preferred_element_type=jnp.float32).astype(
                jnp.bfloat16
            )
            carried = lax.dot_general(
                back_low, entry_a, contract_last, preferred_element_type=jnp.float32
            )
            emitted = (current.astype(jnp.float32) + carried).astype(jnp.bfloat16)
            current = shifted(emitted, "section", -1)
    own_low = project_low(own_grad)
    rows_owned = master.shape[2]
    bucket_rows = rows_owned * lax.axis_size("dp")
    contract_first = (((0,), (0,)), ((), ()))
    masters_list = []
    moments_list = []
    seconds_list = []
    pieces = []
    for bucket in range(BUCKETS):
        offset = bucket * bucket_rows

        def bucket_term(start, count, offset=offset):
            columns = lax.dynamic_slice_in_dim(hidden, offset, count, 1)
            return lax.dot_general(
                columns, own_low, contract_first, preferred_element_type=jnp.float32
            )

        shard_grad = lax.psum_scatter(
            bucket_term(jnp.int32(0), rows_owned * lax.axis_size("dp")),
            "dp",
            scatter_dimension=0,
            tiled=True,
        )
        weights_new, first_new, second_new = adamw(
            shard_grad, master[0, bucket], moment[0, bucket], second[0, bucket]
        )
        masters_list.append(weights_new)
        moments_list.append(first_new)
        seconds_list.append(second_new)
        pieces.append(lax.all_gather(weights_new.astype(jnp.bfloat16), "dp", axis=0, tiled=True))
    weights_new = jnp.stack(masters_list)
    first_new = jnp.stack(moments_list)
    second_new = jnp.stack(seconds_list)
    weight_rows = jnp.concatenate(pieces, axis=0)
    return (weight_rows[None], weights_new[None], first_new[None], second_new[None])


def solution(mesh):
    return jax.shard_map(
        per_device,
        mesh=mesh,
        in_specs=(
            P("dp", "section"),
            P("section", "dp", None),
            P("section", None, None),
            P("section", None, None),
            P("section", None, None),
            P("section", None, None),
            P("section", None, "dp", None),
            P("section", None, "dp", None),
            P("section", None, "dp", None),
        ),
        out_specs=(
            P("section", None, None),
            P("section", None, "dp", None),
            P("section", None, "dp", None),
            P("section", None, "dp", None),
        ),
        check_vma=False,
    )
```

profile of v0, /device:TPU:1, one launch (start us, length us, event | category | flops | bytes accessed | tf_op | source)
XLA Modules:
  0.0 589.1 jit_solution(13049837904330362056)
XLA Ops:
  8.0 31.9 %all-gather.6.cloned.1.call-done = bf16[128,5120]{1,0:T(8,128)(2,1)} async-done(((bf16[128,1280]{1,0:T(8,128)(2,1)}), bf16[128,5120]{1,0:T(8,128)(2,1)}) %all-gather.6.cloned.1.call-update) | async-done | bytes 1310736 | tf_op jit(solution)/shard_map/all_gather | solution.py:38
  39.9 1.9 convolution_convert_fusion.2
  41.8 10.0 %fusion.42 = bf16[128,32]{0,1:T(8,128)(2,1)S(1)} fusion(bf16[1,27648,32]{1,2,0:T(8,128)(2,1)S(1)} %copy-done, bf16[128,32]{0,1:T(8,128)(2,1)S(1)} %convolution_convert_fusion.2, bf16[1,27648,32]{1,2,0:T(8,128)(2,1)} %param.11, bf16[1,128,27648]{2,1,0:T(8,128)(2,1)} %param.10), kind=kOutput, calls=%fused_computation.50 | convolution fusion | flops 488378368 | bytes 10633216 | tf_op jit(solution)/shard_map/dot_general | solution.py:66
  51.9 1.5 fusion.9
  53.4 1.6 collective-permute-start
  55.0 28.7 %collective-permute-done = bf16[128,5120]{1,0:T(8,128)(2,1)S(1)} collective-permute-done((bf16[128,5120]{1,0:T(8,128)(2,1)S(1)}, bf16[128,5120]{1,0:T(8,128)(2,1)S(1)}, u32[]{:S(2)}, u32[]{:S(2)}) %collective-permute-start) | collective-permute-done | bytes 1310752 | tf_op jit(solution)/shard_map/ppermute | solution.py:18
  85.3 9.9 %fusion.47 = bf16[128,32]{0,1:T(8,128)(2,1)S(1)} fusion(bf16[1,27648,32]{1,2,0:T(8,128)(2,1)S(1)} %copy-done, bf16[128,32]{0,1:T(8,128)(2,1)S(1)} %convolution_convert_fusion.1, bf16[1,27648,32]{1,2,0:T(8,128)(2,1)} %param.11, bf16[1,128,27648]{2,1,0:T(8,128)(2,1)} %param.10), kind=kOutput, calls=%fused_computation.51 | convolution fusion | flops 488378368 | bytes 10633216 | tf_op jit(solution)/shard_map/dot_general | solution.py:66
  95.2 2.0 add_convert_fusion.1
  97.2 1.8 collective-permute-start.1
  99.1 28.4 %collective-permute-done.1 = bf16[128,5120]{1,0:T(8,128)(2,1)S(1)} collective-permute-done((bf16[128,5120]{1,0:T(8,128)(2,1)S(1)}, bf16[128,5120]{1,0:T(8,128)(2,1)S(1)}, u32[]{:S(2)}, u32[]{:S(2)}) %collective-permute-start.1) | collective-permute-done | bytes 1310752 | tf_op jit(solution)/shard_map/ppermute | solution.py:18
  129.1 9.9 %fusion.52 = bf16[128,32]{0,1:T(8,128)(2,1)S(1)} fusion(bf16[1,27648,32]{1,2,0:T(8,128)(2,1)S(1)} %copy-done, bf16[128,32]{0,1:T(8,128)(2,1)S(1)} %convolution_convert_fusion, bf16[1,27648,32]{1,2,0:T(8,128)(2,1)} %param.11, bf16[1,128,27648]{2,1,0:T(8,128)(2,1)} %param.10), kind=kOutput, calls=%fused_computation.52 | convolution fusion | flops 488378368 | bytes 10633216 | tf_op jit(solution)/shard_map/dot_general | solution.py:66
  139.0 3.1 add_convert_fusion
  142.1 1.5 collective-permute-start.2
  143.6 9.6 %fusion.6 = bf16[128,27648]{1,0:T(8,128)(2,1)} fusion(bf16[1,128,27648]{2,1,0:T(8,128)(2,1)} %param.10), kind=kLoop, calls=%fused_computation.12 | loop fusion | flops 21233664 | bytes 14155776 | tf_op jit(solution)/shard_map/convert_element_type | solution.py:42
  153.2 18.8 %collective-permute-done.2 = bf16[128,5120]{1,0:T(8,128)(2,1)} collective-permute-done((bf16[128,5120]{1,0:T(8,128)(2,1)}, bf16[128,5120]{1,0:T(8,128)(2,1)}, u32[]{:S(2)}, u32[]{:S(2)}) %collective-permute-start.2) | collective-permute-done | bytes 1310752 | tf_op jit(solution)/shard_map/ppermute | solution.py:18
  172.0 1.8 fusion.39
  180.3 194.1 %all-reduce.7.cloned.1.call-done = (f32[6912,32]{0,1:T(8,128)}, f32[6912,32]{0,1:T(8,128)}, f32[6912,32]{0,1:T(8,128)}, f32[6912,32]{0,1:T(8,128)}) async-done(((f32[6912,32]{0,1:T(8,128)}, f32[6912,32]{0,1:T(8,128)}, f32[6912,32]{0,1:T(8,128)}, f32[6912,32]{0,1:T(8,128)}), (f32[6912,32]{0,1:T(8,128)}, f32[6912,32]{0,1:T(8,128)}, f32[6912,32]{0,1:T(8,128)}, ...) | async-done | bytes 3538960
  376.2 50.7 %all-gather.1 = bf16[64,108,32]{1,2,0:T(8,128)(2,1)S(1)} all-gather(bf16[1,108,32]{1,2,0:T(8,128)(2,1)S(1)} %get-tuple-element.30), channel_id=1, replica_groups=mesh['section'=4,'dp'=64] {'dp'}, dimensions={0}, use_global_device_ids=true | all-gather | bytes 449280 | tf_op jit(solution)/shard_map/all_gather | solution.py:103
  427.9 48.7 %all-gather.2 = bf16[64,108,32]{1,2,0:T(8,128)(2,1)S(1)} all-gather(bf16[1,108,32]{1,2,0:T(8,128)(2,1)S(1)} %get-tuple-element.26), channel_id=1, replica_groups=mesh['section'=4,'dp'=64] {'dp'}, dimensions={0}, use_global_device_ids=true | all-gather | bytes 449280 | tf_op jit(solution)/shard_map/all_gather | solution.py:103
  477.7 48.6 %all-gather.3 = bf16[64,108,32]{1,2,0:T(8,128)(2,1)S(1)} all-gather(bf16[1,108,32]{1,2,0:T(8,128)(2,1)S(1)} %get-tuple-element.14), channel_id=1, replica_groups=mesh['section'=4,'dp'=64] {'dp'}, dimensions={0}, use_global_device_ids=true | all-gather | bytes 449280 | tf_op jit(solution)/shard_map/all_gather | solution.py:103
  526.5 1.5 reshape.34
  528.0 48.5 %all-gather = bf16[64,108,32]{1,2,0:T(8,128)(2,1)S(1)} all-gather(bf16[1,108,32]{1,2,0:T(8,128)(2,1)S(1)} %get-tuple-element.8), channel_id=1, replica_groups=mesh['section'=4,'dp'=64] {'dp'}, dimensions={0}, use_global_device_ids=true | all-gather | bytes 449280 | tf_op jit(solution)/shard_map/all_gather | solution.py:103
  576.7 1.5 reshape.28
  578.9 2.5 maximum_bitcast_fusion
  (41 shorter events, 15.4 us)
Async XLA Ops:
  7.2 34.6 %copy-start = (bf16[1,27648,32]{1,2,0:T(8,128)(2,1)S(1)}, bf16[1,27648,32]{1,2,0:T(8,128)(2,1)}, u32[]{:S(2)}) copy-start(bf16[1,27648,32]{1,2,0:T(8,128)(2,1)} %param.14) | copy-start | bytes 5308420
  7.2 32.7 %all-gather.6.cloned.1.call-start = ((), (), s32[]{:S(2)}) async-start(), calls=%async_computation | async-start | bytes 1638400 | tf_op jit(solution)/shard_map/all_gather | solution.py:38
  7.9 366.5 %all-reduce.7.cloned.1.call-start = ((), (), s32[]{:S(2)}) async-start(), calls=%async_computation.1 | async-start | bytes 7077888
  41.8 10.0 %copy-start.2 = (bf16[128,5120]{1,0:T(8,128)(2,1)S(1)}, bf16[128,5120]{1,0:T(8,128)(2,1)}, u32[]{:S(2)}) copy-start(bf16[128,5120]{1,0:T(8,128)(2,1)} %all-gather.6.cloned.1.call-done) | copy-start | bytes 3932164
  51.9 32.9 %copy-start.5 = (bf16[1,32,5120]{2,1,0:T(8,128)(2,1)S(1)}, bf16[1,32,5120]{2,1,0:T(8,128)(2,1)}, u32[]{:S(2)}) copy-start(bf16[1,32,5120]{2,1,0:T(8,128)(2,1)} %param.12) | copy-start | bytes 983044
  53.4 30.3 %collective-permute-start = (bf16[128,5120]{1,0:T(8,128)(2,1)S(1)}, bf16[128,5120]{1,0:T(8,128)(2,1)S(1)}, u32[]{:S(2)}, u32[]{:S(2)}) collective-permute-start(bf16[128,5120]{1,0:T(8,128)(2,1)S(1)} %fusion.9), channel_id=1, source_target_pairs={{64,0},{128,64},{192,128},{65,1},{129,65},{193,129},{66,2},{130,66... | collective-permute-start | bytes 3932168 | tf_op jit(solution)/shard_map/ppermute | solution.py:18
  83.7 1.1 copy-start.3
  97.2 30.2 %collective-permute-start.1 = (bf16[128,5120]{1,0:T(8,128)(2,1)S(1)}, bf16[128,5120]{1,0:T(8,128)(2,1)S(1)}, u32[]{:S(2)}, u32[]{:S(2)}) collective-permute-start(bf16[128,5120]{1,0:T(8,128)(2,1)S(1)} %add_convert_fusion.1), channel_id=1, source_target_pairs={{64,0},{128,64},{192,128},{65,1},{129,65},{193,129},{66,2},{130,66... | collective-permute-start | bytes 3932168 | tf_op jit(solution)/shard_map/ppermute | solution.py:18
  127.5 1.1 copy-start.4
  142.1 29.9 %collective-permute-start.2 = (bf16[128,5120]{1,0:T(8,128)(2,1)}, bf16[128,5120]{1,0:T(8,128)(2,1)}, u32[]{:S(2)}, u32[]{:S(2)}) collective-permute-start(bf16[128,5120]{1,0:T(8,128)(2,1)} %add_convert_fusion), channel_id=1, source_target_pairs={{64,0},{128,64},{192,128},{65,1},{129,65},{193,129},{66,2},{130,66... | collective-permute-start | bytes 3932168 | tf_op jit(solution)/shard_map/ppermute | solution.py:18
  153.2 20.6 %copy-start.1 = (bf16[128,27648]{1,0:T(8,128)(2,1)S(1)}, bf16[128,27648]{1,0:T(8,128)(2,1)}, u32[]{:S(2)}) copy-start(bf16[128,27648]{1,0:T(8,128)(2,1)} %fusion.6) | copy-start | bytes 21233668
  177.8 1.3 copy-start.9
  177.8 196.7 %copy-start.6 = (f32[1,4,108,32]{2,3,1,0:T(8,128)S(1)}, f32[1,4,108,32]{2,3,1,0:T(8,128)}, u32[]{:S(2)}) copy-start(f32[1,4,108,32]{2,3,1,0:T(8,128)} %param.17) | copy-start | bytes 165892
  177.8 196.7 %copy-start.7 = (f32[1,4,108,32]{2,3,1,0:T(8,128)S(1)}, f32[1,4,108,32]{2,3,1,0:T(8,128)}, u32[]{:S(2)}) copy-start(f32[1,4,108,32]{2,3,1,0:T(8,128)} %param.16) | copy-start | bytes 165892
  177.8 196.7 %copy-start.8 = (f32[1,4,108,32]{2,3,1,0:T(8,128)S(1)}, f32[1,4,108,32]{2,3,1,0:T(8,128)}, u32[]{:S(2)}) copy-start(f32[1,4,108,32]{2,3,1,0:T(8,128)} %param.15) | copy-start | bytes 165892
Sparse Core Ops, SparseCore 0:
  9.8 30.0 all-gather.5
  179.2 195.1 all-reduce.6
where the time goes:
time: 595 us; the launch traced here: 589 us
  waiting for transfers between devices  303 us (51%)
  blocking collectives  197 us (33%)
  matrix products  46.4 us (8%)
  other arithmetic  15.2 us (3%)
  between operations  15.1 us (3%)
  local copies, waits for them, and re-layouts  8.34 us (1%)
    all_gather x4, blocking collectives, per_device(): lax.all_gather(weights_new.astype(jnp.bfloat16), 'dp', axis=0, tiled=True)  197 us
    unnamed x3, waiting for transfers between devices  195 us
    ppermute x3, waiting for transfers between devices, shifted(): lax.ppermute(value, axis, [(source, source + steps) for source in range(i...  75.9 us
    all_gather x1, waiting for transfers between devices, per_device(): top_grad = lax.all_gather(out_grad, 'section', axis=1, tiled=True)  31.9 us
    dot_general x3, matrix products, per_device(): jnp.dot(delta, entry_b, preferred_element_type=jnp.float32)  29.8 us
  transfers between devices with their start and end apart: 5, of which 5 were waited for; matrix products, arithmetic and copies ran while one was open for 2% of the time, Pallas kernels for 0%

commit v1 on v0

--- a/solution.py
+++ b/solution.py
@@ -35,7 +35,24 @@
 
 
 def per_device(out_grad, pre_act, down_a, down_b, up_a, up_b, master, moment, second):
-    top_grad = lax.all_gather(out_grad, "section", axis=1, tiled=True)
+    ways, here, step = (lax.axis_size("section"), lax.axis_index("section"), out_grad.shape[1])
+    dims = [n * ways if d == 1 else n for d, n in enumerate(out_grad.shape)]
+    top_grad = lax.dynamic_update_slice_in_dim(
+        jnp.zeros(dims, out_grad.dtype), out_grad, here * step, axis=1
+    )
+    going_up = going_down = out_grad
+    for far in range(1, ways // 2 + 1):
+        going_up = lax.ppermute(going_up, "section", [(d, (d + 1) % ways) for d in range(ways)])
+        top_grad = lax.dynamic_update_slice_in_dim(
+            top_grad, going_up, (here - far) % ways * step, axis=1
+        )
+        if 2 * far < ways:
+            going_down = lax.ppermute(
+                going_down, "section", [(d, (d - 1) % ways) for d in range(ways)]
+            )
+            top_grad = lax.dynamic_update_slice_in_dim(
+                top_grad, going_down, (here + far) % ways * step, axis=1
+            )
     section_pos = lax.axis_index("section")
     section_count = lax.axis_size("section")
     inputs = pre_act[0].astype(jnp.float32)

time: 595 us -> 581 us (0.976)
  waiting for transfers between devices: 303 us -> 279 us
    all_gather x1 -> x0, waiting for transfers between devices: 31.9 us -> none  [per_device(): top_grad = lax.all_gather(out_grad, 'section', axis=1, tiled=True)]
    ppermute x0 -> x3, waiting for transfers between devices: none -> 8.86 us  [the longest x2 8.85 us: per_device(): lax.ppermute(going_up, 'section', [(d, (d + 1) % ways) for d in range(way...]
    unnamed x3 -> x2, waiting for transfers between devices: 195 us -> 198 us
  transfers between devices with their start and end apart: 5 -> 7, of which waited for: 5 -> 6; matrix products, arithmetic and copies ran while one was open for 2% -> 2% of each run, Pallas kernels for 0% -> 0%
where the time goes in v1:
time: 581 us; the launch traced here: 573 us
  waiting for transfers between devices  279 us (48%)
  blocking collectives  197 us (34%)
  matrix products  44.9 us (8%)
  other arithmetic  15.2 us (3%)
  between operations  15.1 us (3%)
  local copies, waits for them, and re-layouts  12.1 us (2%)
  starting transfers between devices  10.2 us (2%)
    unnamed x2, waiting for transfers between devices  198 us
    all_gather x4, blocking collectives, per_device(): lax.all_gather(weights_new.astype(jnp.bfloat16), 'dp', axis=0, tiled=True)  197 us
    ppermute x3, waiting for transfers between devices, shifted(): lax.ppermute(value, axis, [(source, source + steps) for source in range(i...  72 us
    dot_general x3, matrix products, per_device(): jnp.dot(delta, entry_b, preferred_element_type=jnp.float32)  29.7 us
  transfers between devices with their start and end apart: 7, of which 6 were waited for; matrix products, arithmetic and copies ran while one was open for 2% of the time, Pallas kernels for 0%

profile of v1, /device:TPU:1, one launch (start us, length us, event | category | flops | bytes accessed | tf_op | source)
XLA Modules:
  0.0 573.3 jit_solution(13333307377721276658)
XLA Ops:
  7.2 2.1 collective-permute-start
  11.9 4.2 collective-permute-done
  16.1 1.9 collective-permute-start.2
  20.0 4.7 collective-permute-done.2
  25.3 9.9 %fusion.41 = bf16[128,32]{0,1:T(8,128)(2,1)S(1)} fusion(bf16[1,27648,32]{1,2,0:T(8,128)(2,1)S(1)} %copy-done, bf16[128,32]{0,1:T(8,128)(2,1)S(1)} %convolution_convert_fusion.2, bf16[1,27648,32]{1,2,0:T(8,128)(2,1)} %param.11, bf16[1,128,27648]{2,1,0:T(8,128)(2,1)} %param.10), kind=kOutput, calls=%fused_computation.49 | convolution fusion | flops 488378368 | bytes 10633216 | tf_op jit(solution)/shard_map/dot_general | solution.py:83
  35.2 1.6 add_convert_fusion.2
  36.7 1.6 collective-permute-start.3
  38.3 26.9 %collective-permute-done.3 = bf16[128,5120]{1,0:T(8,128)(2,1)S(1)} collective-permute-done((bf16[128,5120]{1,0:T(8,128)(2,1)S(1)}, bf16[128,5120]{1,0:T(8,128)(2,1)S(1)}, u32[]{:S(2)}, u32[]{:S(2)}) %collective-permute-start.3) | collective-permute-done | bytes 1310752 | tf_op jit(solution)/shard_map/ppermute | solution.py:18
  66.8 9.9 %fusion.46 = bf16[128,32]{0,1:T(8,128)(2,1)S(1)} fusion(bf16[1,27648,32]{1,2,0:T(8,128)(2,1)S(1)} %copy-done, bf16[128,32]{0,1:T(8,128)(2,1)S(1)} %convolution_convert_fusion.1, bf16[1,27648,32]{1,2,0:T(8,128)(2,1)} %param.11, bf16[1,128,27648]{2,1,0:T(8,128)(2,1)} %param.10), kind=kOutput, calls=%fused_computation.50 | convolution fusion | flops 488378368 | bytes 10633216 | tf_op jit(solution)/shard_map/dot_general | solution.py:83
  76.7 2.0 add_convert_fusion.1
  78.7 1.8 collective-permute-start.4
  80.5 27.7 %collective-permute-done.4 = bf16[128,5120]{1,0:T(8,128)(2,1)S(1)} collective-permute-done((bf16[128,5120]{1,0:T(8,128)(2,1)S(1)}, bf16[128,5120]{1,0:T(8,128)(2,1)S(1)}, u32[]{:S(2)}, u32[]{:S(2)}) %collective-permute-start.4) | collective-permute-done | bytes 1310752 | tf_op jit(solution)/shard_map/ppermute | solution.py:18
  109.9 9.9 %fusion.51 = bf16[128,32]{0,1:T(8,128)(2,1)S(1)} fusion(bf16[1,27648,32]{1,2,0:T(8,128)(2,1)S(1)} %copy-done, bf16[128,32]{0,1:T(8,128)(2,1)S(1)} %convolution_convert_fusion, bf16[1,27648,32]{1,2,0:T(8,128)(2,1)} %param.11, bf16[1,128,27648]{2,1,0:T(8,128)(2,1)} %param.10), kind=kOutput, calls=%fused_computation.51 | convolution fusion | flops 488378368 | bytes 10633216 | tf_op jit(solution)/shard_map/dot_general | solution.py:83
  119.8 3.1 add_convert_fusion
  124.3 9.7 %fusion.6 = bf16[128,27648]{1,0:T(8,128)(2,1)} fusion(bf16[1,128,27648]{2,1,0:T(8,128)(2,1)} %param.10), kind=kLoop, calls=%fused_computation.12 | loop fusion | flops 21233664 | bytes 14155776 | tf_op jit(solution)/shard_map/convert_element_type | solution.py:59
  134.0 17.4 %collective-permute-done.5 = bf16[128,5120]{1,0:T(8,128)(2,1)} collective-permute-done((bf16[128,5120]{1,0:T(8,128)(2,1)}, bf16[128,5120]{1,0:T(8,128)(2,1)}, u32[]{:S(2)}, u32[]{:S(2)}) %collective-permute-start.5) | collective-permute-done | bytes 1310752 | tf_op jit(solution)/shard_map/ppermute | solution.py:18
  151.4 1.8 fusion.38
  160.3 198.3 %all-reduce.7.cloned.1.call-done = (f32[6912,32]{0,1:T(8,128)}, f32[6912,32]{0,1:T(8,128)}, f32[6912,32]{0,1:T(8,128)}, f32[6912,32]{0,1:T(8,128)}) async-done(((f32[6912,32]{0,1:T(8,128)}, f32[6912,32]{0,1:T(8,128)}, f32[6912,32]{0,1:T(8,128)}, f32[6912,32]{0,1:T(8,128)}), (f32[6912,32]{0,1:T(8,128)}, f32[6912,32]{0,1:T(8,128)}, f32[6912,32]{0,1:T(8,128)}, ...) | async-done | bytes 3538960
  360.4 50.7 %all-gather.1 = bf16[64,108,32]{1,2,0:T(8,128)(2,1)S(1)} all-gather(bf16[1,108,32]{1,2,0:T(8,128)(2,1)S(1)} %get-tuple-element.30), channel_id=1, replica_groups=mesh['section'=4,'dp'=64] {'dp'}, dimensions={0}, use_global_device_ids=true | all-gather | bytes 449280 | tf_op jit(solution)/shard_map/all_gather | solution.py:120
  412.2 48.7 %all-gather.2 = bf16[64,108,32]{1,2,0:T(8,128)(2,1)S(1)} all-gather(bf16[1,108,32]{1,2,0:T(8,128)(2,1)S(1)} %get-tuple-element.26), channel_id=1, replica_groups=mesh['section'=4,'dp'=64] {'dp'}, dimensions={0}, use_global_device_ids=true | all-gather | bytes 449280 | tf_op jit(solution)/shard_map/all_gather | solution.py:120
  461.9 48.6 %all-gather.3 = bf16[64,108,32]{1,2,0:T(8,128)(2,1)S(1)} all-gather(bf16[1,108,32]{1,2,0:T(8,128)(2,1)S(1)} %get-tuple-element.14), channel_id=1, replica_groups=mesh['section'=4,'dp'=64] {'dp'}, dimensions={0}, use_global_device_ids=true | all-gather | bytes 449280 | tf_op jit(solution)/shard_map/all_gather | solution.py:120
  510.7 1.5 reshape.34
  512.2 48.5 %all-gather = bf16[64,108,32]{1,2,0:T(8,128)(2,1)S(1)} all-gather(bf16[1,108,32]{1,2,0:T(8,128)(2,1)S(1)} %get-tuple-element.8), channel_id=1, replica_groups=mesh['section'=4,'dp'=64] {'dp'}, dimensions={0}, use_global_device_ids=true | all-gather | bytes 449280 | tf_op jit(solution)/shard_map/all_gather | solution.py:120
  563.1 2.5 maximum_bitcast_fusion
  (47 shorter events, 23.2 us)
Async XLA Ops:
  7.2 18.1 %copy-start = (bf16[1,27648,32]{1,2,0:T(8,128)(2,1)S(1)}, bf16[1,27648,32]{1,2,0:T(8,128)(2,1)}, u32[]{:S(2)}) copy-start(bf16[1,27648,32]{1,2,0:T(8,128)(2,1)} %param.14) | copy-start | bytes 5308420
  7.2 351.5 %all-reduce.7.cloned.1.call-start = ((), (), s32[]{:S(2)}) async-start(), calls=%async_computation | async-start | bytes 7077888
  7.2 8.8 %collective-permute-start = (bf16[128,1280]{1,0:T(8,128)(2,1)}, bf16[128,1280]{1,0:T(8,128)(2,1)}, u32[]{:S(2)}, u32[]{:S(2)}) collective-permute-start(bf16[128,1280]{1,0:T(8,128)(2,1)} %param.9), channel_id=1, source_target_pairs={{0,64},{64,128},{128,192},{192,0},{1,65},{65,129},{129,193},{193,1... | collective-permute-start | bytes 983048 | tf_op jit(solution)/shard_map/ppermute | solution.py:45
  9.3 9.6 %collective-permute-start.1 = (bf16[128,1280]{1,0:T(8,128)(2,1)}, bf16[128,1280]{1,0:T(8,128)(2,1)}, u32[]{:S(2)}, u32[]{:S(2)}) collective-permute-start(bf16[128,1280]{1,0:T(8,128)(2,1)} %param.9), channel_id=1, source_target_pairs={{0,192},{64,0},{128,64},{192,128},{1,193},{65,1},{129,65},{193,129... | collective-permute-start | bytes 983048 | tf_op jit(solution)/shard_map/ppermute | solution.py:50
  10.7 14.0 %copy-start.4 = (bf16[1,32,5120]{2,1,0:T(8,128)(2,1)S(1)}, bf16[1,32,5120]{2,1,0:T(8,128)(2,1)}, u32[]{:S(2)}) copy-start(bf16[1,32,5120]{2,1,0:T(8,128)(2,1)} %param.12) | copy-start | bytes 983044
  16.1 8.6 %collective-permute-start.2 = (bf16[128,1280]{1,0:T(8,128)(2,1)}, bf16[128,1280]{1,0:T(8,128)(2,1)S(1)}, u32[]{:S(2)}, u32[]{:S(2)}) collective-permute-start(bf16[128,1280]{1,0:T(8,128)(2,1)} %collective-permute-done), channel_id=1, source_target_pairs={{0,64},{64,128},{128,192},{192,0},{1,65},{65,129},{129,193},{193,1... | collective-permute-start | bytes 983048 | tf_op jit(solution)/shard_map/ppermute | solution.py:45
  36.7 28.5 %collective-permute-start.3 = (bf16[128,5120]{1,0:T(8,128)(2,1)S(1)}, bf16[128,5120]{1,0:T(8,128)(2,1)S(1)}, u32[]{:S(2)}, u32[]{:S(2)}) collective-permute-start(bf16[128,5120]{1,0:T(8,128)(2,1)S(1)} %add_convert_fusion.2), channel_id=1, source_target_pairs={{64,0},{128,64},{192,128},{65,1},{129,65},{193,129},{66,2},{130,66... | collective-permute-start | bytes 3932168 | tf_op jit(solution)/shard_map/ppermute | solution.py:18
  65.2 1.1 copy-start.2
  78.7 29.6 %collective-permute-start.4 = (bf16[128,5120]{1,0:T(8,128)(2,1)S(1)}, bf16[128,5120]{1,0:T(8,128)(2,1)S(1)}, u32[]{:S(2)}, u32[]{:S(2)}) collective-permute-start(bf16[128,5120]{1,0:T(8,128)(2,1)S(1)} %add_convert_fusion.1), channel_id=1, source_target_pairs={{64,0},{128,64},{192,128},{65,1},{129,65},{193,129},{66,2},{130,66... | collective-permute-start | bytes 3932168 | tf_op jit(solution)/shard_map/ppermute | solution.py:18
  108.3 1.1 copy-start.3
  122.9 28.5 %collective-permute-start.5 = (bf16[128,5120]{1,0:T(8,128)(2,1)}, bf16[128,5120]{1,0:T(8,128)(2,1)}, u32[]{:S(2)}, u32[]{:S(2)}) collective-permute-start(bf16[128,5120]{1,0:T(8,128)(2,1)} %add_convert_fusion), channel_id=1, source_target_pairs={{64,0},{128,64},{192,128},{65,1},{129,65},{193,129},{66,2},{130,66... | collective-permute-start | bytes 3932168 | tf_op jit(solution)/shard_map/ppermute | solution.py:18
  134.0 19.2 %copy-start.1 = (bf16[128,27648]{1,0:T(8,128)(2,1)S(1)}, bf16[128,27648]{1,0:T(8,128)(2,1)}, u32[]{:S(2)}) copy-start(bf16[128,27648]{1,0:T(8,128)(2,1)} %fusion.6) | copy-start | bytes 21233668
  158.4 0.7 copy-start.8
  158.4 200.2 %copy-start.5 = (f32[1,4,108,32]{2,3,1,0:T(8,128)S(1)}, f32[1,4,108,32]{2,3,1,0:T(8,128)}, u32[]{:S(2)}) copy-start(f32[1,4,108,32]{2,3,1,0:T(8,128)} %param.17) | copy-start | bytes 165892
  158.4 200.2 %copy-start.6 = (f32[1,4,108,32]{2,3,1,0:T(8,128)S(1)}, f32[1,4,108,32]{2,3,1,0:T(8,128)}, u32[]{:S(2)}) copy-start(f32[1,4,108,32]{2,3,1,0:T(8,128)} %param.16) | copy-start | bytes 165892
  158.4 200.2 %copy-start.7 = (f32[1,4,108,32]{2,3,1,0:T(8,128)S(1)}, f32[1,4,108,32]{2,3,1,0:T(8,128)}, u32[]{:S(2)}) copy-start(f32[1,4,108,32]{2,3,1,0:T(8,128)} %param.15) | copy-start | bytes 165892
Sparse Core Ops, SparseCore 0:
  158.6 200.0 all-reduce.6
